TPU v7x, 32 devices: a whole 2x2x4 slice. The times are simulated.
32 devices in a mesh: stn: 8 (over z, x), chan: 4 (over y, core).
Axes of the slice: x: 2, y: 2, z: 4, core: 2. Of those that a mesh axis runs over, the one named last changes fastest.
Arguments:
- samples: bfloat16 [64, 17, 2, 8192], P(('stn', 'chan')), may hold values from -6 to 6
- keeper: int32 [8, 8], replicated, may hold values from 0 to 1, as said below
Outputs:
- visibilities: bfloat16 [64, 2, 4096, 40], P('stn', None, 'chan')
Inputs may be any that keep to these rules, and one draw needn't show every extreme that they name: keeper[g, g] is 1; for g != h with d = (g - h) mod 8: keeper[g, h] is 1 where 0 < d < 4, 0 where d > 4, and at d = 4 exactly one of keeper[g, h] and keeper[h, g] is 1, which one drawn for each such pair; half of the rows hold 5 ones, the others 5 - 1.
All inputs are finite; a program needn't handle non-finite values.
Results may differ from a plain program's by a relative error of at most 0.0077.
Values may be sent and summed in bfloat16 or wider, within the bound.
A program may use at most 192 MiB of HBM per device.

v0:
```python
import math

import jax
import jax.numpy as jnp
import numpy as np
from jax import lax
from jax.experimental import pallas as pl
from jax.experimental.pallas import tpu as pltpu
from jax.sharding import PartitionSpec as P

TAPS = 16
LANES = 128
CH_WIN = 1024
HIGH = lax.Precision.HIGHEST
OUT_SPACE = pl.ANY


def tables(nfft, n_k2):
    n_1 = nfft // LANES
    pos = np.arange(TAPS * nfft, dtype=np.float64)
    window = 0.5 - 0.5 * np.cos(2.0 * np.pi * (pos + 0.5) / (TAPS * nfft))
    taps = np.sinc((pos + 0.5) / nfft - TAPS / 2.0) * window
    taps = np.repeat(taps.reshape(TAPS, n_1, LANES), 2, axis=1)
    k_1 = np.arange(n_1)
    n_2 = np.arange(LANES)
    angle = 2.0 * np.pi * (k_1[:, None] * k_1[None, :] % n_1) / n_1
    cosine, sine = np.cos(angle), np.sin(angle)
    first = np.zeros((2, n_1, n_1, 2))
    first[0, :, :, 0] = cosine
    first[0, :, :, 1] = sine
    first[1, :, :, 0] = -sine
    first[1, :, :, 1] = cosine
    first = first.reshape(2 * n_1, 2 * n_1)
    angle = 2.0 * np.pi * (n_2[:, None] * k_1[None, :] % nfft) / nfft
    scale = 1.0 / math.sqrt(nfft)
    turn_c = np.concatenate([np.cos(angle), np.cos(angle)], axis=1) * scale
    turn_s = np.concatenate([np.sin(angle), -np.sin(angle)], axis=1) * scale
    k_2 = np.concatenate([np.arange(0, n_k2, 2), np.arange(1, n_k2, 2)])
    angle = 2.0 * np.pi * (k_2[:, None] * n_2[None, :] % LANES) / LANES
    second = np.concatenate([np.cos(angle), np.sin(angle)], axis=1)
    return [np.asarray(a, np.float32) for a in (taps, first, turn_c, turn_s, second)]


def filter_rows(x_ref, taps_ref, held, inputs, frames):
    rows = taps_ref.shape[1]
    chunk = 16
    for start in range(0, rows, chunk):
        part = slice(start, start + chunk)
        for i in range(inputs):
            totals = [None] * frames
            for step in range(TAPS + frames - 1):
                value = x_ref[i, step, part, :].astype(jnp.float32)
                for f in range(frames):
                    if 0 <= step - f < TAPS:
                        term = value * taps_ref[step - f, part, :]
                        totals[f] = term if totals[f] is None else totals[f] + term
            for f in range(frames):
                seq = i * frames + f
                held[part, seq * LANES : (seq + 1) * LANES] = totals[f]


def transform(held, first_ref, turn_c_ref, turn_s_ref, second_ref, seqs):
    half = LANES // 2
    stage = jnp.dot(first_ref[...], held[...], precision=HIGH, preferred_element_type=jnp.float32)
    lane = lax.broadcasted_iota(jnp.int32, (LANES, LANES), 1)
    sign = jnp.where(lane < half, 1.0, -1.0)
    tops, lows = [], []
    for seq in range(seqs):
        turned = stage[:, seq * LANES : (seq + 1) * LANES].T
        turned = turned * turn_c_ref[...] + pltpu.roll(turned, half, 1) * turn_s_ref[...]
        tops.append(turned)
        lows.append(pltpu.roll(turned, half, 1) * sign)
    rhs = jnp.concatenate([jnp.concatenate(tops, axis=1), jnp.concatenate(lows, axis=1)], axis=0)
    spectra = jnp.dot(second_ref[...], rhs, precision=HIGH, preferred_element_type=jnp.float32)
    tiles = spectra.shape[0] // 2
    low_lane = lax.broadcasted_iota(jnp.int32, (tiles, LANES), 1) < half
    planes = []
    for seq in range(seqs):
        even = spectra[:tiles, seq * LANES : (seq + 1) * LANES]
        odd = spectra[tiles:, seq * LANES : (seq + 1) * LANES]
        real = jnp.where(low_lane, even, pltpu.roll(odd, half, 1))
        imag = jnp.where(low_lane, pltpu.roll(even, half, 1), odd)
        planes.append((real, imag))
    return planes


def send_kernel(
    x_ref, taps_ref, first_ref, turn_c_ref, turn_s_ref, second_ref, parts_ref, held, mine, here_sem, send_sem, pass_sem, recv_sem
):
    n_chan, inputs, frames, _, tiles, _ = mine.shape
    n_stn = lax.axis_size("stn")
    hops = (parts_ref.shape[0] - 1) // 2
    stn = lax.axis_index("stn")
    chan = lax.axis_index("chan")
    odd = lax.rem(stn, 2)
    pair = stn + 1 - 2 * odd

    barrier = pltpu.get_barrier_semaphore()
    for j in range(hops + 1):
        for step in range(n_chan):
            if j or step:
                there = (lax.rem(stn + n_stn - 2 * j, n_stn), lax.rem(chan + step, n_chan))
                pl.semaphore_signal(barrier, inc=1, device_id=there, device_id_type=pl.DeviceIdType.MESH)
    pl.semaphore_signal(barrier, inc=1, device_id=(pair, chan), device_id_type=pl.DeviceIdType.MESH)

    filter_rows(x_ref, taps_ref, held, inputs, frames)
    planes = transform(held, first_ref, turn_c_ref, turn_s_ref, second_ref, inputs * frames)
    for i in range(inputs):
        for f in range(frames):
            for p in range(2):
                plane = planes[i * frames + f][p].astype(jnp.bfloat16)
                for d in range(n_chan):
                    mine[d, i, f, p] = plane[d * tiles : (d + 1) * tiles]
    pl.semaphore_wait(barrier, (hops + 1) * n_chan)

    def direct(j, step):
        to = lax.rem(chan + step, n_chan)
        return pltpu.make_async_remote_copy(
            src_ref=mine.at[to],
            dst_ref=parts_ref.at[2 * j, chan],
            send_sem=send_sem.at[j, step],
            recv_sem=recv_sem.at[2 * j, chan],
            device_id=(lax.rem(stn + 2 * j, n_stn), to),
            device_id_type=pl.DeviceIdType.MESH,
        )

    def arrival(distance, origin):
        return pltpu.make_async_remote_copy(
            src_ref=mine.at[0],
            dst_ref=parts_ref.at[distance, origin],
            send_sem=send_sem.at[0, 0],
            recv_sem=recv_sem.at[distance, origin],
            device_id=(pair, chan),
            device_id_type=pl.DeviceIdType.MESH,
        )

    def passed(j, step):
        origin = lax.rem(chan + step, n_chan)
        return pltpu.make_async_remote_copy(
            src_ref=parts_ref.at[2 * (j + odd), origin],
            dst_ref=parts_ref.at[2 * j + 1, origin],
            send_sem=pass_sem.at[j, step],
            recv_sem=recv_sem.at[2 * j + 1, origin],
            device_id=(pair, chan),
            device_id_type=pl.DeviceIdType.MESH,
        )

    keep = pltpu.make_async_copy(mine.at[chan], parts_ref.at[0, chan], here_sem)
    keep.start()
    for step in range(n_chan):
        for j in range(hops, -1, -1):
            if j or step:
                direct(j, step).start()
    keep.wait()
    for j in range(hops + 1):
        for step in range(n_chan):
            if j or step:
                arrival(2 * j, lax.rem(chan + n_chan - step, n_chan)).wait_recv()
        first = j == 0
        last = j == hops

        @pl.when(odd == 0)
        def _():
            if not last:
                for step in range(n_chan):
                    passed(j, step).start()

        @pl.when(odd == 1)
        def _():
            if not first:
                for step in range(n_chan):
                    passed(j - 1, step).start()

    for j in range(hops):
        for step in range(n_chan):
            arrival(2 * j + 1, lax.rem(chan + step, n_chan)).wait_recv()
            passed(j, step).wait_send()
    for j in range(hops + 1):
        for step in range(n_chan):
            if j or step:
                direct(j, step).wait_send()


def channelise(samples, n_chan, half):
    inputs, frames_in, _, nfft = samples.shape
    frames = frames_in - TAPS + 1
    tiles = CH_WIN // LANES
    n_1 = nfft // LANES
    consts = tables(nfft, CH_WIN * n_chan // n_1)
    x = samples.reshape(inputs, frames_in, 2, n_1, LANES)
    x = jnp.transpose(x, (0, 1, 3, 2, 4)).reshape(inputs, frames_in, 2 * n_1, LANES)
    piece = (n_chan, inputs, frames, 2, tiles, LANES)
    return pl.pallas_call(
        send_kernel,
        out_shape=jax.ShapeDtypeStruct((half + 1,) + piece, jnp.bfloat16),
        in_specs=[pl.BlockSpec(memory_space=pltpu.VMEM)] * 6,
        out_specs=pl.BlockSpec(memory_space=OUT_SPACE),
        scratch_shapes=[
            pltpu.VMEM((2 * n_1, inputs * frames * LANES), jnp.float32),
            pltpu.VMEM(piece, jnp.bfloat16),
            pltpu.SemaphoreType.DMA,
            pltpu.SemaphoreType.DMA((half // 2 + 1, n_chan)),
            pltpu.SemaphoreType.DMA((half // 2, n_chan)),
            pltpu.SemaphoreType.DMA((half + 1, n_chan)),
        ],
        compiler_params=pltpu.CompilerParams(collective_id=0, has_side_effects=True),
        name="channelise",
    )(x, *consts)


def correlate_kernel(keeper_ref, parts_ref, out_ref, own, others, dist, gain):
    step = pl.program_id(0)
    _, n_chan, pieces, frames, _, tiles, _ = parts_ref.shape
    inputs = n_chan * pieces
    pieces = out_ref.shape[0]
    slots = parts_ref.shape[0]
    n_stn = keeper_ref.shape[0]

    @pl.when(step == 0)
    def _():
        group = lax.axis_index("stn")
        for s in range(slots):
            dist[s] = 0
            gain[s] = jnp.float32(0.0)

        def place(h, rank):
            kept = keeper_ref[group, h] == 1

            @pl.when(kept & (rank < slots))
            def _():
                dist[rank] = jnp.minimum(lax.rem(group + n_stn - h, n_stn), slots - 1)
                gain[rank] = jnp.float32(1.0 / frames)

            return rank + kept.astype(jnp.int32)

        lax.fori_loop(0, n_stn, place, jnp.int32(0))

        for f in range(frames):
            for p in range(2):
                value = parts_ref[0, :, :, f, p].astype(jnp.float32).reshape(inputs, tiles, LANES)
                own[f, p] = jnp.transpose(value, (1, 0, 2))
                for s in range(slots):
                    value = parts_ref[dist[s], :, :, f, p].astype(jnp.float32) * gain[s]
                    value = value.reshape(inputs, tiles, LANES)
                    others[f, p, s] = jnp.transpose(value, (1, 0, 2))

    for t in range(tiles):
        rows = []
        for i in range(pieces):
            rows.append([
                [jnp.broadcast_to(own[f, p, t, pl.ds(step * pieces + i, 1), :], (inputs, LANES)) for p in range(2)]
                for f in range(frames)
            ])
        for s in range(slots):
            block = [[others[f, p, s, t] for p in range(2)] for f in range(frames)]
            for i in range(pieces):
                real, imag = 0.0, 0.0
                for f in range(frames):
                    a_re, a_im = rows[i][f]
                    b_re, b_im = block[f]
                    real = real + (a_re * b_re + a_im * b_im)
                    imag = imag + (a_im * b_re - a_re * b_im)
                top = slice(s * inputs, (s + 1) * inputs)
                col = slice(t * LANES, (t + 1) * LANES)
                out_ref[i, 0, top, col] = real.astype(jnp.bfloat16)
                out_ref[i, 1, top, col] = imag.astype(jnp.bfloat16)


def correlate(keeper, parts):
    slots, n_chan, pieces, frames, _, tiles, _ = parts.shape
    inputs = n_chan * pieces
    out = pl.pallas_call(
        correlate_kernel,
        out_shape=jax.ShapeDtypeStruct((inputs, 2, slots * inputs, tiles * LANES), jnp.bfloat16),
        grid=(2,),
        in_specs=[
            pl.BlockSpec(memory_space=pltpu.SMEM),
            pl.BlockSpec(parts.shape, lambda t: (0,) * 7),
        ],
        out_specs=pl.BlockSpec((inputs // 2, 2, slots * inputs, tiles * LANES), lambda t: (t, 0, 0, 0)),
        scratch_shapes=[
            pltpu.VMEM((frames, 2, tiles, inputs, LANES), jnp.float32),
            pltpu.VMEM((frames, 2, slots, tiles, inputs, LANES), jnp.float32),
            pltpu.SMEM((slots,), jnp.int32),
            pltpu.SMEM((slots,), jnp.float32),
        ],
        name="correlate",
    )(keeper, parts)
    return jnp.transpose(out, (0, 1, 3, 2))


def per_device(samples, keeper):
    half = lax.axis_size("stn") // 2
    return correlate(keeper, channelise(samples, lax.axis_size("chan"), half))


def solution(mesh):
    placed = (P(("stn", "chan"), None, None, None), P())
    return jax.shard_map(
        per_device,
        mesh=mesh,
        in_specs=placed,
        out_specs=P("stn", None, "chan", None),
        check_vma=False,
    )
```

profile of v0, /device:TPU:0, one launch (start us, length us, event | category | flops | bytes accessed | tf_op | source)
XLA Modules:
  0.0 21.3 jit_solution(5999508366966820523)
XLA Ops:
  0.0 18.5 %channelise.1.parts_ref = bf16[5,4,2,2,2,8,128]{6,5,4,3,2,1,0:T(8,128)(2,1)} custom-call(bf16[2,17,128,128]{3,2,1,0:T(8,128)(2,1)} %bitcast.6, f32[16,128,128]{2,1,0:T(8,128)} %constant.10.clone.taps_ref, f32[128,128]{1,0:T(8,128)} %constant.11.clone.first_ref, f32[128,128]{1,0:T(8,128)} %constant.12.clone.turn_c_ref, f32[128,128]{1,0:T(8,128)} %constant.13.clone.turn_s_ref, ...), custom_call_target="tpu_custom_call" | custom-call | tf_op jit(solution)/shard_map/channelise/pallas_call | solution.py:193
  18.5 2.8 %correlate.1 = bf16[8,2,40,1024]{3,2,1,0:T(8,128)(2,1)} custom-call(s32[8,8]{1,0:T(8,128)} %keeper_ref.1, bf16[5,4,2,2,2,8,128]{6,5,4,3,2,1,0:T(8,128)(2,1)} %channelise.1.parts_ref), custom_call_target="tpu_custom_call" | custom-call | tf_op jit(solution)/shard_map/correlate/pallas_call | solution.py:272
where the time goes:
time: 21.5 us; the launch traced here: 21.3 us
  Pallas kernels  21.3 us (99%)
    pallas_call x1, Pallas kernels, channelise(): pl.pallas_call(send_kernel, out_shape=jax.ShapeDtypeStruct((half + 1,) +...  18.5 us
    pallas_call x1, Pallas kernels, correlate(): pl.pallas_call(correlate_kernel, out_shape=jax.ShapeDtypeStruct((inputs,...  2.83 us

commit v1 on v0

v1 whole, which is shorter than its diff:
```python
import math

import jax
import jax.numpy as jnp
import numpy as np
from jax import lax
from jax.experimental import pallas as pl
from jax.experimental.pallas import tpu as pltpu
from jax.sharding import PartitionSpec as P

TAPS = 16
LANES = 128
CH_WIN = 1024
HIGH = lax.Precision.HIGHEST
MESH = pl.DeviceIdType.MESH
VMEM_LIMIT = 24 << 20
CHUNKS = 4


def tables(nfft, n_k2):
    n_1 = nfft // LANES
    pos = np.arange(TAPS * nfft, dtype=np.float64)
    window = 0.5 - 0.5 * np.cos(2.0 * np.pi * (pos + 0.5) / (TAPS * nfft))
    taps = np.sinc((pos + 0.5) / nfft - TAPS / 2.0) * window
    taps = np.repeat(taps.reshape(TAPS, n_1, LANES), 2, axis=1)
    k_1 = np.arange(n_1)
    n_2 = np.arange(LANES)
    angle = 2.0 * np.pi * (k_1[:, None] * k_1[None, :] % n_1) / n_1
    cosine, sine = np.cos(angle), np.sin(angle)
    first = np.zeros((2, n_1, n_1, 2))
    first[0, :, :, 0] = cosine
    first[0, :, :, 1] = sine
    first[1, :, :, 0] = -sine
    first[1, :, :, 1] = cosine
    first = first.reshape(2 * n_1, 2 * n_1)
    angle = 2.0 * np.pi * (n_2[:, None] * k_1[None, :] % nfft) / nfft
    scale = 1.0 / math.sqrt(nfft)
    turn_c = np.concatenate([np.cos(angle), np.cos(angle)], axis=1) * scale
    turn_s = np.concatenate([np.sin(angle), -np.sin(angle)], axis=1) * scale
    k_2 = np.concatenate([np.arange(0, n_k2, 2), np.arange(1, n_k2, 2)])
    angle = 2.0 * np.pi * (k_2[:, None] * n_2[None, :] % LANES) / LANES
    second = np.concatenate([np.cos(angle), np.sin(angle)], axis=1)
    return [np.asarray(a, np.float32) for a in (taps, first, turn_c, turn_s, second)]


def filter_rows(x_ref, taps_ref, held, first_row, rows, inputs, frames):
    chunk = 16
    for start in range(first_row, first_row + rows, chunk):
        part = slice(start, start + chunk)
        for i in range(inputs):
            totals = [None] * frames
            for step in range(TAPS + frames - 1):
                value = x_ref[i, step, part, :].astype(jnp.float32)
                for f in range(frames):
                    if 0 <= step - f < TAPS:
                        term = value * taps_ref[step - f, part, :]
                        totals[f] = term if totals[f] is None else totals[f] + term
            for f in range(frames):
                seq = i * frames + f
                held[part, seq * LANES : (seq + 1) * LANES] = totals[f]


def transform(held, first_ref, turn_c_ref, turn_s_ref, second_ref, seqs):
    half = LANES // 2
    stage = jnp.dot(first_ref[...], held[...], precision=HIGH, preferred_element_type=jnp.float32)
    lane = lax.broadcasted_iota(jnp.int32, (LANES, LANES), 1)
    sign = jnp.where(lane < half, 1.0, -1.0)
    tops, lows = [], []
    for seq in range(seqs):
        turned = stage[:, seq * LANES : (seq + 1) * LANES].T
        turned = turned * turn_c_ref[...] + pltpu.roll(turned, half, 1) * turn_s_ref[...]
        tops.append(turned)
        lows.append(pltpu.roll(turned, half, 1) * sign)
    rhs = jnp.concatenate([jnp.concatenate(tops, axis=1), jnp.concatenate(lows, axis=1)], axis=0)
    spectra = jnp.dot(second_ref[...], rhs, precision=HIGH, preferred_element_type=jnp.float32)
    tiles = spectra.shape[0] // 2
    low_lane = lax.broadcasted_iota(jnp.int32, (tiles, LANES), 1) < half
    planes = []
    for seq in range(seqs):
        even = spectra[:tiles, seq * LANES : (seq + 1) * LANES]
        odd = spectra[tiles:, seq * LANES : (seq + 1) * LANES]
        real = jnp.where(low_lane, even, pltpu.roll(odd, half, 1))
        imag = jnp.where(low_lane, pltpu.roll(even, half, 1), odd)
        planes.append((real, imag))
    return planes


WRAP_FROM_ODD = True
WRAP_FROM_EVEN = False
AHEAD_FROM_ODD = False
AHEAD_FROM_EVEN = False


def both(flag, cond):
    return cond if flag else jnp.bool_(False)


def straight(source, d, n_stn):
    wraps = source + d >= n_stn
    odd = lax.rem(source, 2) == 1
    from_odd = both(WRAP_FROM_ODD, wraps) | both(AHEAD_FROM_ODD, ~wraps)
    from_even = both(WRAP_FROM_EVEN, wraps) | both(AHEAD_FROM_EVEN, ~wraps) | (d == 1)
    return (lax.rem(d, 2) == 0) | (odd & from_odd) | (~odd & from_even)


def kernel(
    keeper_ref, x_ref, taps_ref, first_ref, turn_c_ref, turn_s_ref, second_ref, out_ref,
    x_in, taps_in, first_in, turn_c_in, turn_s_in, second_in, keeper_in,
    held, mine, parts, own, others,
    x_sem, taps_sem, const_sem, send_sem, pass_sem, recv_sem,
):
    n_chan, inputs, frames, _, tiles, _ = mine.shape
    n_stn = keeper_ref.shape[0]
    half = parts.shape[0] - 1
    slots = half + 1
    group = n_chan * inputs
    stn = lax.axis_index("stn")
    chan = lax.axis_index("chan")
    odd = lax.rem(stn, 2)
    pair = stn + 1 - 2 * odd
    rows = held.shape[0] // CHUNKS

    loads = []
    for c in range(CHUNKS):
        part = pl.ds(c * rows, rows)
        loads.append((
            pltpu.make_async_copy(x_ref.at[:, :, part], x_in.at[:, :, part], x_sem.at[c]),
            pltpu.make_async_copy(taps_ref.at[:, part], taps_in.at[:, part], taps_sem.at[c]),
        ))
    consts = [
        pltpu.make_async_copy(source, target, const_sem.at[q])
        for q, (source, target) in enumerate([
            (first_ref, first_in), (turn_c_ref, turn_c_in), (turn_s_ref, turn_s_in),
            (second_ref, second_in), (keeper_ref, keeper_in),
        ])
    ]
    for pair_of in loads:
        for load in pair_of:
            load.start()
    for load in consts:
        load.start()

    barrier = pltpu.get_barrier_semaphore()

    def greet(d, carry):
        for step in range(n_chan):
            @pl.when((d > 0) | (step > 0))
            def _():
                there = (lax.rem(stn + n_stn - d, n_stn), lax.rem(chan + step, n_chan))
                pl.semaphore_signal(barrier, inc=1, device_id=there, device_id_type=MESH)
        return carry

    lax.fori_loop(0, half + 1, greet, 0)

    @pl.when(odd == 0)
    def _():
        pl.semaphore_signal(barrier, inc=1, device_id=(pair, chan), device_id_type=MESH)

    for c in range(CHUNKS):
        for load in loads[c]:
            load.wait()
        filter_rows(x_in, taps_in, held, c * rows, rows, inputs, frames)
    for load in consts:
        load.wait()
    planes = transform(held, first_in, turn_c_in, turn_s_in, second_in, inputs * frames)
    for i in range(inputs):
        for f in range(frames):
            for p in range(2):
                plane = planes[i * frames + f][p].astype(jnp.bfloat16)
                for d in range(n_chan):
                    mine[d, i, f, p] = plane[d * tiles : (d + 1) * tiles]
    parts[0, chan] = mine[chan]
    pl.semaphore_wait(barrier, (half + 1) * n_chan - 1 + odd)

    first_wrap = n_stn - stn
    first_far = jnp.where(first_wrap <= half, first_wrap, 1)

    def target(step):
        core = lax.rem(chan, 2)
        return 2 * (step // 2) + lax.rem(core + step, 2)

    def direct(d, step):
        to = target(step)
        return pltpu.make_async_remote_copy(
            src_ref=mine.at[to],
            dst_ref=parts.at[d, chan],
            send_sem=send_sem.at[d, step],
            recv_sem=recv_sem.at[d, chan],
            device_id=(lax.rem(stn + d, n_stn), to),
            device_id_type=MESH,
        )

    def passed(d, origin):
        return pltpu.make_async_remote_copy(
            src_ref=parts.at[d, origin],
            dst_ref=parts.at[d + 1 - 2 * odd, origin],
            send_sem=pass_sem.at[d, origin],
            recv_sem=recv_sem.at[d + 1 - 2 * odd, origin],
            device_id=(pair, chan),
            device_id_type=MESH,
        )

    def passes(d):
        later = d + 1 - 2 * odd
        source = lax.rem(stn + n_stn - d, n_stn)
        return (lax.rem(d, 2) == 0) & (later > 0) & (later < half) & ~straight(source, later, n_stn)

    def far(k):
        return lax.rem(first_far - 1 + k, half) + 1

    def send(k, carry):
        d = far(k)

        @pl.when(straight(stn, d, n_stn))
        def _():
            for step in range(n_chan):
                direct(d, step).start()

        return carry

    lax.fori_loop(0, half, send, 0)
    for step in range(n_chan):
        @pl.when(target(step) != chan)
        def _():
            direct(0, step).start()

    away = lax.rem(stn + half, n_stn)
    row = keeper_in[pl.ds(stn, 1), :]
    column = lax.broadcasted_iota(jnp.int32, row.shape, 1)
    kept = jnp.max(jnp.where(column == away, row, 0), axis=1, keepdims=True)
    kept = jnp.broadcast_to(kept, (group, LANES)) == 1
    base = jnp.where(stn < half, stn + 1, 0)

    def rank(d):
        there = jnp.where(odd == 0, lax.div(half - 1 - d, 2), lax.div(d - 1, 2))
        even = jnp.where(d == 0, 0, 1 + lax.div(half - d, 2))
        return jnp.where(lax.rem(d, 2) == 0, even, half // 2 + 1 + there)

    def at_rank(k):
        odds = k - (half // 2 + 1)
        late = jnp.where(odd == 0, half - 1 - 2 * odds, 1 + 2 * odds)
        even = jnp.where(k == 0, 0, half - 2 * (k - 1))
        return jnp.where(k <= half // 2, even, late)

    def receive(k, carry):
        d = at_rank(k)
        for origin in range(n_chan):
            @pl.when((d > 0) | (origin != chan))
            def _():
                pltpu.make_async_remote_copy(
                    src_ref=mine.at[0],
                    dst_ref=parts.at[d, origin],
                    send_sem=send_sem.at[0, 0],
                    recv_sem=recv_sem.at[d, origin],
                    device_id=(pair, chan),
                    device_id_type=MESH,
                ).wait_recv()

            @pl.when(passes(d))
            def _():
                passed(d, origin).start()

        for f in range(frames):
            for p in range(2):
                value = parts[d, :, :, f, p].astype(jnp.float32).reshape(group, tiles, LANES)
                others[d, f, p] = jnp.transpose(value, (1, 0, 2))

        @pl.when(k == 0)
        def _():
            for f in range(frames):
                for p in range(2):
                    own[f, p] = others[0, f, p] * (1.0 / frames)

        def slot(s, inner):
            single = s < base
            with_far = jnp.where(single, stn - s, half + base - s)
            unfilled = (s == half) & ~single
            without = jnp.where(single | unfilled, with_far, with_far - 1)
            gain = jnp.where(unfilled, 0.0, 1.0).astype(jnp.float32)
            ready = jnp.maximum(rank(with_far), rank(without))

            @pl.when(ready == k)
            def _():
                for t in range(tiles):
                    block = [
                        [jnp.where(kept, others[with_far, f, p, t], others[without, f, p, t] * gain) for p in range(2)]
                        for f in range(frames)
                    ]
                    for i in range(group):
                        real, imag = 0.0, 0.0
                        for f in range(frames):
                            a_re, a_im = [jnp.broadcast_to(own[f, p, t, pl.ds(i, 1), :], (group, LANES)) for p in range(2)]
                            b_re, b_im = block[f]
                            real = real + (a_re * b_re + a_im * b_im)
                            imag = imag + (a_im * b_re - a_re * b_im)
                        lanes = slice(t * LANES, (t + 1) * LANES)
                        out_ref[i, 0, s, :, lanes] = real.astype(jnp.bfloat16)
                        out_ref[i, 1, s, :, lanes] = imag.astype(jnp.bfloat16)

            return inner

        lax.fori_loop(0, slots, slot, 0)
        return carry

    lax.fori_loop(0, half + 1, receive, 0)

    def finish(d, carry):
        @pl.when(straight(stn, d, n_stn))
        def _():
            for step in range(n_chan):
                direct(d, step).wait_send()

        @pl.when(passes(d))
        def _():
            for origin in range(n_chan):
                passed(d, origin).wait_send()

        return carry

    lax.fori_loop(1, half + 1, finish, 0)
    for step in range(n_chan):
        @pl.when(target(step) != chan)
        def _():
            direct(0, step).wait_send()


def per_device(samples, keeper):
    n_stn, n_chan = lax.axis_size("stn"), lax.axis_size("chan")
    inputs, frames_in, _, nfft = samples.shape
    half = n_stn // 2
    frames = frames_in - TAPS + 1
    tiles = CH_WIN // LANES
    n_1 = nfft // LANES
    group = n_chan * inputs
    consts = tables(nfft, CH_WIN * n_chan // n_1)
    x = samples.reshape(inputs, frames_in, 2, n_1, LANES)
    x = jnp.transpose(x, (0, 1, 3, 2, 4)).reshape(inputs, frames_in, 2 * n_1, LANES)
    piece = (n_chan, inputs, frames, 2, tiles, LANES)
    dma = pltpu.SemaphoreType.DMA
    out = pl.pallas_call(
        kernel,
        out_shape=jax.ShapeDtypeStruct((group, 2, half + 1, group, tiles * LANES), jnp.bfloat16),
        in_specs=[pl.BlockSpec(memory_space=pltpu.HBM)] * 7,
        out_specs=pl.BlockSpec(memory_space=pltpu.VMEM),
        scratch_shapes=[
            pltpu.VMEM(x.shape, x.dtype),
            *[pltpu.VMEM(a.shape, jnp.float32) for a in consts],
            pltpu.VMEM(keeper.shape, keeper.dtype),
            pltpu.VMEM((2 * n_1, inputs * frames * LANES), jnp.float32),
            pltpu.VMEM(piece, jnp.bfloat16),
            pltpu.VMEM((half + 1,) + piece, jnp.bfloat16),
            pltpu.VMEM((frames, 2, tiles, group, LANES), jnp.float32),
            pltpu.VMEM((half + 1, frames, 2, tiles, group, LANES), jnp.float32),
            dma((CHUNKS,)),
            dma((CHUNKS,)),
            dma((5,)),
            dma((half + 1, n_chan)),
            dma((half + 1, n_chan)),
            dma((half + 1, n_chan)),
        ],
        compiler_params=pltpu.CompilerParams(collective_id=0, has_side_effects=True, vmem_limit_bytes=VMEM_LIMIT),
        name="correlator",
    )(*[pltpu.with_memory_space_constraint(a, pltpu.HBM) for a in (keeper, x, *[jnp.asarray(c) for c in consts])])
    out = out.reshape(group, 2, (half + 1) * group, tiles * LANES)
    return jnp.transpose(out, (0, 1, 3, 2))


def solution(mesh):
    placed = (P(("stn", "chan"), None, None, None), P())
    return jax.shard_map(
        per_device,
        mesh=mesh,
        in_specs=placed,
        out_specs=P("stn", None, "chan", None),
        check_vma=False,
    )
```

time: 21.5 us -> 19.3 us (0.90)
  Pallas kernels: 21.3 us -> 18.1 us
  local copies, waits for them, and re-layouts: 0 us -> 1.06 us
    pallas_call x2 -> x1, Pallas kernels: 21.3 us -> 18.1 us  [per_device(): pl.pallas_call(kernel, out_shape=jax.ShapeDtypeStruct((group, 2, half + 1...]
    unnamed x0 -> x1, local copies, waits for them, and re-layouts: none -> 1.06 us
where the time goes in v1:
time: 19.3 us; the launch traced here: 19.2 us
  Pallas kernels  18.1 us (94%)
  local copies, waits for them, and re-layouts  1.06 us (5%)
    pallas_call x1, Pallas kernels, per_device(): pl.pallas_call(kernel, out_shape=jax.ShapeDtypeStruct((group, 2, half + 1...  18.1 us
    unnamed x1, local copies, waits for them, and re-layouts  1.06 us

profile of v1, /device:TPU:0, one launch (start us, length us, event | category | flops | bytes accessed | tf_op | source)
XLA Modules:
  0.0 19.2 jit_solution(15924852708245946078)
XLA Ops:
  0.0 18.1 %correlator.1 = bf16[8,2,5,8,1024]{4,3,2,1,0:T(8,128)(2,1)S(1)} custom-call(s32[8,8]{1,0:T(8,128)} %keeper_ref.1, bf16[2,17,128,128]{3,2,1,0:T(8,128)(2,1)} %bitcast.9, f32[16,128,128]{2,1,0:T(8,128)} %constant.10.clone.taps_ref, f32[128,128]{1,0:T(8,128)} %constant.11.clone.first_ref, f32[128,128]{1,0:T(8,128)} %constant.12.clone.turn_c_ref, ...), custom_call_target="tpu_custom_call" | custom-call | tf_op jit(solution)/shard_map/correlator/pallas_call | solution.py:340
  18.1 1.1 %copy.10 = bf16[8,2,1024,40]{2,3,1,0:T(8,128)(2,1)} copy(bf16[8,2,1024,40]{2,3,1,0:T(8,128)(2,1)S(1)} %bitcast.8) | data formatting | bytes 2621440

commit v2 on v1

--- a/solution.py
+++ b/solution.py
@@ -11,7 +11,6 @@
 TAPS = 16
 LANES = 128
 CH_WIN = 1024
-HIGH = lax.Precision.HIGHEST
 MESH = pl.DeviceIdType.MESH
 VMEM_LIMIT = 24 << 20
 CHUNKS = 4
@@ -40,7 +39,14 @@
     k_2 = np.concatenate([np.arange(0, n_k2, 2), np.arange(1, n_k2, 2)])
     angle = 2.0 * np.pi * (k_2[:, None] * n_2[None, :] % LANES) / LANES
     second = np.concatenate([np.cos(angle), np.sin(angle)], axis=1)
-    return [np.asarray(a, np.float32) for a in (taps, first, turn_c, turn_s, second)]
+    first = np.concatenate(halves(first), axis=1)
+    second = np.concatenate(halves(second), axis=0)
+    return [np.asarray(a, np.float32) for a in (taps, turn_c, turn_s)] + [first, second]
+
+
+def halves(table):
+    high = table.astype(jnp.bfloat16)
+    return high, (table - high.astype(np.float64)).astype(jnp.bfloat16)
 
 
 def filter_rows(x_ref, taps_ref, held, first_row, rows, inputs, frames):
@@ -57,57 +63,67 @@
                         totals[f] = term if totals[f] is None else totals[f] + term
             for f in range(frames):
                 seq = i * frames + f
-                held[part, seq * LANES : (seq + 1) * LANES] = totals[f]
+                for q, half in enumerate(split(totals[f])):
+                    held[q, part, seq * LANES : (seq + 1) * LANES] = half
+
+
+def split(value):
+    high = value.astype(jnp.bfloat16)
+    return high, (value - high.astype(jnp.float32)).astype(jnp.bfloat16)
+
+
+def dot(a, b):
+    return jnp.dot(a, b, preferred_element_type=jnp.float32)
 
 
 def transform(held, first_ref, turn_c_ref, turn_s_ref, second_ref, seqs):
     half = LANES // 2
-    stage = jnp.dot(first_ref[...], held[...], precision=HIGH, preferred_element_type=jnp.float32)
+    high = held[0]
+    depth = high.shape[0]
+    stage = dot(first_ref[...], jnp.concatenate([high, high], axis=0)) + dot(first_ref[:, :depth], held[1])
     lane = lax.broadcasted_iota(jnp.int32, (LANES, LANES), 1)
     sign = jnp.where(lane < half, 1.0, -1.0)
-    tops, lows = [], []
+    rows = second_ref.shape[0] // 2
+    planes = []
     for seq in range(seqs):
         turned = stage[:, seq * LANES : (seq + 1) * LANES].T
         turned = turned * turn_c_ref[...] + pltpu.roll(turned, half, 1) * turn_s_ref[...]
-        tops.append(turned)
-        lows.append(pltpu.roll(turned, half, 1) * sign)
-    rhs = jnp.concatenate([jnp.concatenate(tops, axis=1), jnp.concatenate(lows, axis=1)], axis=0)
-    spectra = jnp.dot(second_ref[...], rhs, precision=HIGH, preferred_element_type=jnp.float32)
-    tiles = spectra.shape[0] // 2
-    low_lane = lax.broadcasted_iota(jnp.int32, (tiles, LANES), 1) < half
-    planes = []
-    for seq in range(seqs):
-        even = spectra[:tiles, seq * LANES : (seq + 1) * LANES]
-        odd = spectra[tiles:, seq * LANES : (seq + 1) * LANES]
+        low = pltpu.roll(turned, half, 1) * sign
+        high, rest = split(jnp.concatenate([turned, low], axis=0))
+        product = dot(second_ref[...], high)
+        spectra = product[:rows] + product[rows:] + dot(second_ref[:rows], rest)
+        tiles = rows // 2
+        low_lane = lax.broadcasted_iota(jnp.int32, (tiles, LANES), 1) < half
+        even, odd = spectra[:tiles], spectra[tiles:]
         real = jnp.where(low_lane, even, pltpu.roll(odd, half, 1))
         imag = jnp.where(low_lane, pltpu.roll(even, half, 1), odd)
         planes.append((real, imag))
     return planes
 
 
-WRAP_FROM_ODD = True
-WRAP_FROM_EVEN = False
-AHEAD_FROM_ODD = False
-AHEAD_FROM_EVEN = False
-
-
-def both(flag, cond):
-    return cond if flag else jnp.bool_(False)
+NEAR_WRAP = False
+FAR_WRAP = False
+NEAR_AHEAD = False
+FAR_AHEAD = False
+DOUBLE = False
+GATE = 3
+LAST = 2
 
 
 def straight(source, d, n_stn):
     wraps = source + d >= n_stn
     odd = lax.rem(source, 2) == 1
-    from_odd = both(WRAP_FROM_ODD, wraps) | both(AHEAD_FROM_ODD, ~wraps)
-    from_even = both(WRAP_FROM_EVEN, wraps) | both(AHEAD_FROM_EVEN, ~wraps) | (d == 1)
-    return (lax.rem(d, 2) == 0) | (odd & from_odd) | (~odd & from_even)
+    near = d <= 2
+    to_even = (wraps & ((near & NEAR_WRAP) | (~near & FAR_WRAP))) | (~wraps & ((near & NEAR_AHEAD) | (~near & FAR_AHEAD)))
+    odd_d = lax.rem(d, 2) == 1
+    return (odd & (odd_d == to_even)) | (~odd & (~odd_d | (d == 1))) | (d == 0) | (DOUBLE & odd & wraps & (d == 1))
 
 
 def kernel(
-    keeper_ref, x_ref, taps_ref, first_ref, turn_c_ref, turn_s_ref, second_ref, out_ref,
-    x_in, taps_in, first_in, turn_c_in, turn_s_in, second_in, keeper_in,
+    keeper_ref, x_ref, taps_ref, turn_c_ref, turn_s_ref, first_ref, second_ref, out_ref,
+    x_in, taps_in, turn_c_in, turn_s_in, first_in, second_in, keeper_in,
     held, mine, parts, own, others,
-    x_sem, taps_sem, const_sem, send_sem, pass_sem, recv_sem,
+    x_sem, taps_sem, const_sem, send_sem, pass_sem, recv_sem, here_sem,
 ):
     n_chan, inputs, frames, _, tiles, _ = mine.shape
     n_stn = keeper_ref.shape[0]
@@ -118,7 +134,7 @@
     chan = lax.axis_index("chan")
     odd = lax.rem(stn, 2)
     pair = stn + 1 - 2 * odd
-    rows = held.shape[0] // CHUNKS
+    rows = held.shape[1] // CHUNKS
 
     loads = []
     for c in range(CHUNKS):
@@ -142,24 +158,42 @@
 
     barrier = pltpu.get_barrier_semaphore()
 
-    def greet(d, carry):
+    def signal_all(semaphore, there):
         for step in range(n_chan):
-            @pl.when((d > 0) | (step > 0))
-            def _():
-                there = (lax.rem(stn + n_stn - d, n_stn), lax.rem(chan + step, n_chan))
-                pl.semaphore_signal(barrier, inc=1, device_id=there, device_id_type=MESH)
-        return carry
-
-    lax.fori_loop(0, half + 1, greet, 0)
-
-    @pl.when(odd == 0)
-    def _():
-        pl.semaphore_signal(barrier, inc=1, device_id=(pair, chan), device_id_type=MESH)
+            to = lax.rem(chan + step, n_chan)
+            pl.semaphore_signal(semaphore, inc=1, device_id=(there, to), device_id_type=MESH)
+
+    def enter(d, carry):
+        @pl.when(d > stn)
+        def _():
+            signal_all(barrier, stn - d + n_stn)
+
+        @pl.when(stn + d < n_stn)
+        def _():
+            signal_all(barrier, stn + d)
+
+        return carry
+
+    lax.fori_loop(1, half + 1, enter, 0)
+    for step in range(1, n_chan):
+        there = (stn, lax.rem(chan + step, n_chan))
+        pl.semaphore_signal(barrier, inc=1, device_id=there, device_id_type=MESH)
 
     for c in range(CHUNKS):
         for load in loads[c]:
             load.wait()
         filter_rows(x_in, taps_in, held, c * rows, rows, inputs, frames)
+    back = jnp.maximum(stn - half + 1, 0)
+    pl.semaphore_wait(barrier, (back + jnp.minimum(stn, half) + 1) * n_chan - 1)
+
+    def answer(d, carry):
+        @pl.when(d <= stn)
+        def _():
+            signal_all(here_sem.at[d], stn - d)
+
+        return carry
+
+    lax.fori_loop(1, half + 1, answer, 0)
     for load in consts:
         load.wait()
     planes = transform(held, first_in, turn_c_in, turn_s_in, second_in, inputs * frames)
@@ -170,10 +204,6 @@
                 for d in range(n_chan):
                     mine[d, i, f, p] = plane[d * tiles : (d + 1) * tiles]
     parts[0, chan] = mine[chan]
-    pl.semaphore_wait(barrier, (half + 1) * n_chan - 1 + odd)
-
-    first_wrap = n_stn - stn
-    first_far = jnp.where(first_wrap <= half, first_wrap, 1)
 
     def target(step):
         core = lax.rem(chan, 2)
@@ -203,26 +233,58 @@
     def passes(d):
         later = d + 1 - 2 * odd
         source = lax.rem(stn + n_stn - d, n_stn)
-        return (lax.rem(d, 2) == 0) & (later > 0) & (later < half) & ~straight(source, later, n_stn)
-
-    def far(k):
-        return lax.rem(first_far - 1 + k, half) + 1
-
-    def send(k, carry):
-        d = far(k)
-
-        @pl.when(straight(stn, d, n_stn))
+        needed = (d > 0) & (later > 0) & (later <= half)
+        return needed & straight(source, d, n_stn) & ~straight(source, later, n_stn)
+
+    def late(d):
+        return stn + d >= n_stn + LAST
+
+    def send(d, carry):
+        @pl.when((stn + d >= n_stn) & ~late(d) & straight(stn, d, n_stn))
         def _():
             for step in range(n_chan):
                 direct(d, step).start()
 
         return carry
 
-    lax.fori_loop(0, half, send, 0)
+    def gates(d):
+        return (stn + half >= n_stn + LAST) & (stn + d >= n_stn) & ~late(d) & straight(stn, d, n_stn)
+
+    def gate(d, carry):
+        @pl.when(gates(d))
+        def _():
+            direct(d, GATE).wait_send()
+
+        return carry
+
+    def send_late(d, carry):
+        @pl.when(late(d) & straight(stn, d, n_stn))
+        def _():
+            for step in range(n_chan):
+                direct(d, step).start()
+
+        return carry
+
+    def send_ahead(d, carry):
+        @pl.when(stn + d < n_stn)
+        def _():
+            pl.semaphore_wait(here_sem.at[d], n_chan)
+
+            @pl.when(straight(stn, d, n_stn))
+            def _():
+                for step in range(n_chan):
+                    direct(d, step).start()
+
+        return carry
+
     for step in range(n_chan):
         @pl.when(target(step) != chan)
         def _():
             direct(0, step).start()
+    lax.fori_loop(1, half + 1, send, 0)
+    lax.fori_loop(1, half + 1, send_ahead, 0)
+    lax.fori_loop(1, half + 1, gate, 0)
+    lax.fori_loop(1, half + 1, send_late, 0)
 
     away = lax.rem(stn + half, n_stn)
     row = keeper_in[pl.ds(stn, 1), :]
@@ -231,19 +293,28 @@
     kept = jnp.broadcast_to(kept, (group, LANES)) == 1
     base = jnp.where(stn < half, stn + 1, 0)
 
+    ahead = jnp.minimum(stn, half)
+
+    def comes_straight(d):
+        return straight(lax.rem(stn + n_stn - d, n_stn), d, n_stn)
+
     def rank(d):
-        there = jnp.where(odd == 0, lax.div(half - 1 - d, 2), lax.div(d - 1, 2))
-        even = jnp.where(d == 0, 0, 1 + lax.div(half - d, 2))
-        return jnp.where(lax.rem(d, 2) == 0, even, half // 2 + 1 + there)
+        place = jnp.where(d <= ahead, d, half + 1 + ahead - d)
+        return jnp.where(comes_straight(d), place, place + slots)
 
     def at_rank(k):
-        odds = k - (half // 2 + 1)
-        late = jnp.where(odd == 0, half - 1 - 2 * odds, 1 + 2 * odds)
-        even = jnp.where(k == 0, 0, half - 2 * (k - 1))
-        return jnp.where(k <= half // 2, even, late)
+        return jnp.where(k <= ahead, k, half + 1 + ahead - k)
 
     def receive(k, carry):
-        d = at_rank(k)
+        d = at_rank(lax.rem(k, slots))
+
+        @pl.when(comes_straight(d) == (k < slots))
+        def _():
+            take(k, d)
+
+        return carry
+
+    def take(k, d):
         for origin in range(n_chan):
             @pl.when((d > 0) | (origin != chan))
             def _():
@@ -300,15 +371,19 @@
             return inner
 
         lax.fori_loop(0, slots, slot, 0)
-        return carry
-
-    lax.fori_loop(0, half + 1, receive, 0)
+
+    lax.fori_loop(0, 2 * slots, receive, 0)
 
     def finish(d, carry):
         @pl.when(straight(stn, d, n_stn))
         def _():
             for step in range(n_chan):
-                direct(d, step).wait_send()
+                if step != GATE:
+                    direct(d, step).wait_send()
+
+        @pl.when(straight(stn, d, n_stn) & ~gates(d))
+        def _():
+            direct(d, GATE).wait_send()
 
         @pl.when(passes(d))
         def _():
@@ -344,9 +419,9 @@
         out_specs=pl.BlockSpec(memory_space=pltpu.VMEM),
         scratch_shapes=[
             pltpu.VMEM(x.shape, x.dtype),
-            *[pltpu.VMEM(a.shape, jnp.float32) for a in consts],
+            *[pltpu.VMEM(a.shape, a.dtype) for a in consts],
             pltpu.VMEM(keeper.shape, keeper.dtype),
-            pltpu.VMEM((2 * n_1, inputs * frames * LANES), jnp.float32),
+            pltpu.VMEM((2, 2 * n_1, inputs * frames * LANES), jnp.bfloat16),
             pltpu.VMEM(piece, jnp.bfloat16),
             pltpu.VMEM((half + 1,) + piece, jnp.bfloat16),
             pltpu.VMEM((frames, 2, tiles, group, LANES), jnp.float32),
@@ -357,6 +432,7 @@
             dma((half + 1, n_chan)),
             dma((half + 1, n_chan)),
             dma((half + 1, n_chan)),
+            pltpu.SemaphoreType.REGULAR((half + 1,)),
         ],
         compiler_params=pltpu.CompilerParams(collective_id=0, has_side_effects=True, vmem_limit_bytes=VMEM_LIMIT),
         name="correlator",

time: 19.3 us -> 17.6 us (0.912)
  Pallas kernels: 18.1 us -> 16.4 us
    pallas_call x1, Pallas kernels: 18.1 us -> 16.4 us  [per_device(): pl.pallas_call(kernel, out_shape=jax.ShapeDtypeStruct((group, 2, half + 1...]
where the time goes in v2:
time: 17.6 us; the launch traced here: 17.4 us
  Pallas kernels  16.4 us (93%)
  local copies, waits for them, and re-layouts  1.06 us (6%)
    pallas_call x1, Pallas kernels, per_device(): pl.pallas_call(kernel, out_shape=jax.ShapeDtypeStruct((group, 2, half + 1...  16.4 us
    unnamed x1, local copies, waits for them, and re-layouts  1.06 us

profile of v2, /device:TPU:0, one launch (start us, length us, event | category | flops | bytes accessed | tf_op | source)
XLA Modules:
  0.0 17.4 jit_solution(2973478181718664128)
XLA Ops:
  0.0 16.4 %correlator.1 = bf16[8,2,5,8,1024]{4,3,2,1,0:T(8,128)(2,1)S(1)} custom-call(s32[8,8]{1,0:T(8,128)} %keeper_ref.1, bf16[2,17,128,128]{3,2,1,0:T(8,128)(2,1)} %bitcast.9, f32[16,128,128]{2,1,0:T(8,128)} %constant.10.clone.taps_ref, f32[128,128]{1,0:T(8,128)} %constant.11.clone.turn_c_ref, f32[128,128]{1,0:T(8,128)} %constant.12.clone.turn_s_ref, ...), custom_call_target="tpu_custom_call" | custom-call | tf_op jit(solution)/shard_map/correlator/pallas_call | solution.py:415
  16.4 1.1 %copy.10 = bf16[8,2,1024,40]{2,3,1,0:T(8,128)(2,1)} copy(bf16[8,2,1024,40]{2,3,1,0:T(8,128)(2,1)S(1)} %bitcast.8) | data formatting | bytes 2621440

commit v3 on v2

--- a/solution.py
+++ b/solution.py
@@ -85,13 +85,17 @@
     sign = jnp.where(lane < half, 1.0, -1.0)
     rows = second_ref.shape[0] // 2
     planes = []
+    his = []
     for seq in range(seqs):
         turned = stage[:, seq * LANES : (seq + 1) * LANES].T
         turned = turned * turn_c_ref[...] + pltpu.roll(turned, half, 1) * turn_s_ref[...]
         low = pltpu.roll(turned, half, 1) * sign
-        high, rest = split(jnp.concatenate([turned, low], axis=0))
-        product = dot(second_ref[...], high)
-        spectra = product[:rows] + product[rows:] + dot(second_ref[:rows], rest)
+        his.append(jnp.concatenate([turned, low], axis=0))
+    high, rest = split(jnp.concatenate(his, axis=1))
+    product = dot(second_ref[...], high)
+    every = product[:rows] + product[rows:] + dot(second_ref[:rows], rest)
+    for seq in range(seqs):
+        spectra = every[:, seq * LANES : (seq + 1) * LANES]
         tiles = rows // 2
         low_lane = lax.broadcasted_iota(jnp.int32, (tiles, LANES), 1) < half
         even, odd = spectra[:tiles], spectra[tiles:]
@@ -101,22 +105,15 @@
     return planes
 
 
-NEAR_WRAP = False
-FAR_WRAP = False
-NEAR_AHEAD = False
-FAR_AHEAD = False
-DOUBLE = False
 GATE = 3
 LAST = 2
 
 
-def straight(source, d, n_stn):
-    wraps = source + d >= n_stn
+def straight(source, origin, d, n_stn):
     odd = lax.rem(source, 2) == 1
-    near = d <= 2
-    to_even = (wraps & ((near & NEAR_WRAP) | (~near & FAR_WRAP))) | (~wraps & ((near & NEAR_AHEAD) | (~near & FAR_AHEAD)))
     odd_d = lax.rem(d, 2) == 1
-    return (odd & (odd_d == to_even)) | (~odd & (~odd_d | (d == 1))) | (d == 0) | (DOUBLE & odd & wraps & (d == 1))
+    to_even = (source + d >= n_stn) & (d > 2) & (lax.rem(origin, 2) == 0)
+    return (odd & (odd_d == to_even)) | (~odd & (~odd_d | (d == 1))) | (d == 0)
 
 
 def kernel(
@@ -183,17 +180,6 @@
         for load in loads[c]:
             load.wait()
         filter_rows(x_in, taps_in, held, c * rows, rows, inputs, frames)
-    back = jnp.maximum(stn - half + 1, 0)
-    pl.semaphore_wait(barrier, (back + jnp.minimum(stn, half) + 1) * n_chan - 1)
-
-    def answer(d, carry):
-        @pl.when(d <= stn)
-        def _():
-            signal_all(here_sem.at[d], stn - d)
-
-        return carry
-
-    lax.fori_loop(1, half + 1, answer, 0)
     for load in consts:
         load.wait()
     planes = transform(held, first_in, turn_c_in, turn_s_in, second_in, inputs * frames)
@@ -230,17 +216,17 @@
             device_id_type=MESH,
         )
 
-    def passes(d):
+    def passes(d, origin):
         later = d + 1 - 2 * odd
         source = lax.rem(stn + n_stn - d, n_stn)
         needed = (d > 0) & (later > 0) & (later <= half)
-        return needed & straight(source, d, n_stn) & ~straight(source, later, n_stn)
+        return needed & straight(source, origin, d, n_stn) & ~straight(source, origin, later, n_stn)
 
     def late(d):
         return stn + d >= n_stn + LAST
 
     def send(d, carry):
-        @pl.when((stn + d >= n_stn) & ~late(d) & straight(stn, d, n_stn))
+        @pl.when((stn + d >= n_stn) & ~late(d) & straight(stn, chan, d, n_stn))
         def _():
             for step in range(n_chan):
                 direct(d, step).start()
@@ -248,7 +234,7 @@
         return carry
 
     def gates(d):
-        return (stn + half >= n_stn + LAST) & (stn + d >= n_stn) & ~late(d) & straight(stn, d, n_stn)
+        return (stn + half >= n_stn + LAST) & (stn + d >= n_stn) & ~late(d) & straight(stn, chan, d, n_stn)
 
     def gate(d, carry):
         @pl.when(gates(d))
@@ -258,7 +244,7 @@
         return carry
 
     def send_late(d, carry):
-        @pl.when(late(d) & straight(stn, d, n_stn))
+        @pl.when(late(d) & straight(stn, chan, d, n_stn))
         def _():
             for step in range(n_chan):
                 direct(d, step).start()
@@ -268,20 +254,42 @@
     def send_ahead(d, carry):
         @pl.when(stn + d < n_stn)
         def _():
-            pl.semaphore_wait(here_sem.at[d], n_chan)
-
-            @pl.when(straight(stn, d, n_stn))
+            pl.semaphore_wait(here_sem.at[d], 1)
+
+            @pl.when(straight(stn, chan, d, n_stn))
             def _():
                 for step in range(n_chan):
                     direct(d, step).start()
 
         return carry
 
+    back = jnp.maximum(stn - half + 1, 0)
+    pl.semaphore_wait(barrier, (back + jnp.minimum(stn, half) + 1) * n_chan - 1)
+
+
+    def answer(d, carry):
+        @pl.when(d <= stn)
+        def _():
+            pl.semaphore_signal(here_sem.at[d], inc=1, device_id=(stn - d, chan), device_id_type=MESH)
+
+        return carry
+
+    lax.fori_loop(1, half + 1, answer, 0)
+    last = stn + half >= n_stn + LAST
+
+    @pl.when(~last)
+    def _():
+        lax.fori_loop(1, half + 1, send, 0)
+
     for step in range(n_chan):
         @pl.when(target(step) != chan)
         def _():
             direct(0, step).start()
-    lax.fori_loop(1, half + 1, send, 0)
+
+    @pl.when(last)
+    def _():
+        lax.fori_loop(1, half + 1, send, 0)
+
     lax.fori_loop(1, half + 1, send_ahead, 0)
     lax.fori_loop(1, half + 1, gate, 0)
     lax.fori_loop(1, half + 1, send_late, 0)
@@ -295,28 +303,28 @@
 
     ahead = jnp.minimum(stn, half)
 
-    def comes_straight(d):
-        return straight(lax.rem(stn + n_stn - d, n_stn), d, n_stn)
+    def comes_straight(d, origin):
+        return straight(lax.rem(stn + n_stn - d, n_stn), origin, d, n_stn)
+
+    def all_straight(d):
+        every = comes_straight(d, 0)
+        for origin in range(1, n_chan):
+            every = every & comes_straight(d, origin)
+        return every
 
     def rank(d):
         place = jnp.where(d <= ahead, d, half + 1 + ahead - d)
-        return jnp.where(comes_straight(d), place, place + slots)
+        return jnp.where(all_straight(d), place, place + slots)
 
     def at_rank(k):
         return jnp.where(k <= ahead, k, half + 1 + ahead - k)
 
     def receive(k, carry):
         d = at_rank(lax.rem(k, slots))
-
-        @pl.when(comes_straight(d) == (k < slots))
-        def _():
-            take(k, d)
-
-        return carry
-
-    def take(k, d):
         for origin in range(n_chan):
-            @pl.when((d > 0) | (origin != chan))
+            here = (d == 0) & (origin == chan)
+
+            @pl.when((comes_straight(d, origin) == (k < slots)) & ~here)
             def _():
                 pltpu.make_async_remote_copy(
                     src_ref=mine.at[0],
@@ -327,10 +335,17 @@
                     device_id_type=MESH,
                 ).wait_recv()
 
-            @pl.when(passes(d))
+            @pl.when((k < slots) & passes(d, origin))
             def _():
                 passed(d, origin).start()
 
+        @pl.when(all_straight(d) == (k < slots))
+        def _():
+            take(k, d)
+
+        return carry
+
+    def take(k, d):
         for f in range(frames):
             for p in range(2):
                 value = parts[d, :, :, f, p].astype(jnp.float32).reshape(group, tiles, LANES)
@@ -375,19 +390,19 @@
     lax.fori_loop(0, 2 * slots, receive, 0)
 
     def finish(d, carry):
-        @pl.when(straight(stn, d, n_stn))
+        @pl.when(straight(stn, chan, d, n_stn))
         def _():
             for step in range(n_chan):
                 if step != GATE:
                     direct(d, step).wait_send()
 
-        @pl.when(straight(stn, d, n_stn) & ~gates(d))
+        @pl.when(straight(stn, chan, d, n_stn) & ~gates(d))
         def _():
             direct(d, GATE).wait_send()
 
-        @pl.when(passes(d))
-        def _():
-            for origin in range(n_chan):
+        for origin in range(n_chan):
+            @pl.when(passes(d, origin))
+            def _():
                 passed(d, origin).wait_send()
 
         return carry

time: 17.6 us -> 16.9 us (0.960)
  Pallas kernels: 16.4 us -> 15.7 us
    pallas_call x1, Pallas kernels: 16.4 us -> 15.7 us  [per_device(): pl.pallas_call(kernel, out_shape=jax.ShapeDtypeStruct((group, 2, half + 1...]
where the time goes in v3:
time: 16.9 us; the launch traced here: 16.8 us
  Pallas kernels  15.7 us (93%)
  local copies, waits for them, and re-layouts  1.06 us (6%)
    pallas_call x1, Pallas kernels, per_device(): pl.pallas_call(kernel, out_shape=jax.ShapeDtypeStruct((group, 2, half + 1...  15.7 us
    unnamed x1, local copies, waits for them, and re-layouts  1.06 us

profile of v3, /device:TPU:0, one launch (start us, length us, event | category | flops | bytes accessed | tf_op | source)
XLA Modules:
  0.0 16.8 jit_solution(954530043352149528)
XLA Ops:
  0.0 15.7 %correlator.1 = bf16[8,2,5,8,1024]{4,3,2,1,0:T(8,128)(2,1)S(1)} custom-call(s32[8,8]{1,0:T(8,128)} %keeper_ref.1, bf16[2,17,128,128]{3,2,1,0:T(8,128)(2,1)} %bitcast.9, f32[16,128,128]{2,1,0:T(8,128)} %constant.10.clone.taps_ref, f32[128,128]{1,0:T(8,128)} %constant.11.clone.turn_c_ref, f32[128,128]{1,0:T(8,128)} %constant.12.clone.turn_s_ref, ...), custom_call_target="tpu_custom_call" | custom-call | tf_op jit(solution)/shard_map/correlator/pallas_call | solution.py:430
  15.7 1.1 %copy.10 = bf16[8,2,1024,40]{2,3,1,0:T(8,128)(2,1)} copy(bf16[8,2,1024,40]{2,3,1,0:T(8,128)(2,1)S(1)} %bitcast.8) | data formatting | bytes 2621440

commit v4 on v3

--- a/solution.py
+++ b/solution.py
@@ -18,10 +18,6 @@
 
 def tables(nfft, n_k2):
     n_1 = nfft // LANES
-    pos = np.arange(TAPS * nfft, dtype=np.float64)
-    window = 0.5 - 0.5 * np.cos(2.0 * np.pi * (pos + 0.5) / (TAPS * nfft))
-    taps = np.sinc((pos + 0.5) / nfft - TAPS / 2.0) * window
-    taps = np.repeat(taps.reshape(TAPS, n_1, LANES), 2, axis=1)
     k_1 = np.arange(n_1)
     n_2 = np.arange(LANES)
     angle = 2.0 * np.pi * (k_1[:, None] * k_1[None, :] % n_1) / n_1
@@ -41,12 +37,47 @@
     second = np.concatenate([np.cos(angle), np.sin(angle)], axis=1)
     first = np.concatenate(halves(first), axis=1)
     second = np.concatenate(halves(second), axis=0)
-    return [np.asarray(a, np.float32) for a in (taps, turn_c, turn_s)] + [first, second]
+    return [np.asarray(a, np.float32) for a in (turn_c, turn_s)] + [first, second]
 
 
 def halves(table):
     high = table.astype(jnp.bfloat16)
     return high, (table - high.astype(np.float64)).astype(jnp.bfloat16)
+
+
+def series(square, terms):
+    total = jnp.full_like(square, terms[-1])
+    for term in reversed(terms[:-1]):
+        total = total * square + term
+    return total
+
+
+def make_taps(taps_ref):
+    rows = taps_ref.shape[1]
+    nfft = rows // 2 * LANES
+    height = 8
+    odd = [(-1) ** q * math.pi ** (2 * q) / math.factorial(2 * q + 1) for q in range(7)]
+    turn = 2.0 * math.pi / TAPS
+    cosine = [(-1) ** q * turn ** (2 * q) / math.factorial(2 * q) for q in range(5)]
+    sine = [(-1) ** q * turn ** (2 * q + 1) / math.factorial(2 * q + 1) for q in range(5)]
+
+    def block(j, carry):
+        start = pl.multiple_of(j * height, height)
+        row = lax.broadcasted_iota(jnp.int32, (height, LANES), 0) + start
+        lane = lax.broadcasted_iota(jnp.int32, (height, LANES), 1)
+        u = (lax.div(row, 2) * LANES + lane).astype(jnp.float32) * (1.0 / nfft) + 0.5 / nfft
+        near = jnp.minimum(u, 1.0 - u)
+        wave = near * series(near * near, odd)
+        square = u * u
+        cos_u, sin_u = series(square, cosine), u * series(square, sine)
+        for t in range(TAPS):
+            sign = -1.0 if t % 2 else 1.0
+            c, s = math.cos(turn * t) * 0.5 * sign, math.sin(turn * t) * 0.5 * sign
+            window = (0.5 * sign - c * cos_u) + s * sin_u
+            taps_ref[t, pl.ds(start, height), :] = wave * window / (u + (t - TAPS // 2))
+        return carry
+
+    lax.fori_loop(0, rows // height, block, 0)
 
 
 def filter_rows(x_ref, taps_ref, held, first_row, rows, inputs, frames):
@@ -117,10 +148,10 @@
 
 
 def kernel(
-    keeper_ref, x_ref, taps_ref, turn_c_ref, turn_s_ref, first_ref, second_ref, out_ref,
+    keeper_ref, x_ref, turn_c_ref, turn_s_ref, first_ref, second_ref, out_ref,
     x_in, taps_in, turn_c_in, turn_s_in, first_in, second_in, keeper_in,
     held, mine, parts, own, others,
-    x_sem, taps_sem, const_sem, send_sem, pass_sem, recv_sem, here_sem,
+    x_sem, const_sem, send_sem, pass_sem, recv_sem, here_sem,
 ):
     n_chan, inputs, frames, _, tiles, _ = mine.shape
     n_stn = keeper_ref.shape[0]
@@ -136,10 +167,7 @@
     loads = []
     for c in range(CHUNKS):
         part = pl.ds(c * rows, rows)
-        loads.append((
-            pltpu.make_async_copy(x_ref.at[:, :, part], x_in.at[:, :, part], x_sem.at[c]),
-            pltpu.make_async_copy(taps_ref.at[:, part], taps_in.at[:, part], taps_sem.at[c]),
-        ))
+        loads.append(pltpu.make_async_copy(x_ref.at[:, :, part], x_in.at[:, :, part], x_sem.at[c]))
     consts = [
         pltpu.make_async_copy(source, target, const_sem.at[q])
         for q, (source, target) in enumerate([
@@ -147,10 +175,7 @@
             (second_ref, second_in), (keeper_ref, keeper_in),
         ])
     ]
-    for pair_of in loads:
-        for load in pair_of:
-            load.start()
-    for load in consts:
+    for load in loads + consts:
         load.start()
 
     barrier = pltpu.get_barrier_semaphore()
@@ -176,9 +201,9 @@
         there = (stn, lax.rem(chan + step, n_chan))
         pl.semaphore_signal(barrier, inc=1, device_id=there, device_id_type=MESH)
 
+    make_taps(taps_in)
     for c in range(CHUNKS):
-        for load in loads[c]:
-            load.wait()
+        loads[c].wait()
         filter_rows(x_in, taps_in, held, c * rows, rows, inputs, frames)
     for load in consts:
         load.wait()
@@ -307,10 +332,9 @@
         return straight(lax.rem(stn + n_stn - d, n_stn), origin, d, n_stn)
 
     def all_straight(d):
-        every = comes_straight(d, 0)
-        for origin in range(1, n_chan):
-            every = every & comes_straight(d, origin)
-        return every
+        source = lax.rem(stn + n_stn - d, n_stn)
+        mixed = (lax.rem(source, 2) == 1) & (d > stn) & (d > 2)
+        return ((lax.rem(d, 2) == 0) & ~mixed) | ((lax.rem(source, 2) == 0) & (d == 1))
 
     def rank(d):
         place = jnp.where(d <= ahead, d, half + 1 + ahead - d)
@@ -387,9 +411,7 @@
 
         lax.fori_loop(0, slots, slot, 0)
 
-    lax.fori_loop(0, 2 * slots, receive, 0)
-
-    def finish(d, carry):
+    def sent(d, carry):
         @pl.when(straight(stn, chan, d, n_stn))
         def _():
             for step in range(n_chan):
@@ -400,6 +422,9 @@
         def _():
             direct(d, GATE).wait_send()
 
+        return carry
+
+    def passed_on(d, carry):
         for origin in range(n_chan):
             @pl.when(passes(d, origin))
             def _():
@@ -407,11 +432,14 @@
 
         return carry
 
-    lax.fori_loop(1, half + 1, finish, 0)
+    lax.fori_loop(0, slots, receive, 0)
+    lax.fori_loop(1, half + 1, sent, 0)
     for step in range(n_chan):
         @pl.when(target(step) != chan)
         def _():
             direct(0, step).wait_send()
+    lax.fori_loop(slots, 2 * slots, receive, 0)
+    lax.fori_loop(1, half + 1, passed_on, 0)
 
 
 def per_device(samples, keeper):
@@ -430,10 +458,11 @@
     out = pl.pallas_call(
         kernel,
         out_shape=jax.ShapeDtypeStruct((group, 2, half + 1, group, tiles * LANES), jnp.bfloat16),
-        in_specs=[pl.BlockSpec(memory_space=pltpu.HBM)] * 7,
+        in_specs=[pl.BlockSpec(memory_space=pltpu.HBM)] * 6,
         out_specs=pl.BlockSpec(memory_space=pltpu.VMEM),
         scratch_shapes=[
             pltpu.VMEM(x.shape, x.dtype),
+            pltpu.VMEM((TAPS, 2 * n_1, LANES), jnp.float32),
             *[pltpu.VMEM(a.shape, a.dtype) for a in consts],
             pltpu.VMEM(keeper.shape, keeper.dtype),
             pltpu.VMEM((2, 2 * n_1, inputs * frames * LANES), jnp.bfloat16),
@@ -441,7 +470,6 @@
             pltpu.VMEM((half + 1,) + piece, jnp.bfloat16),
             pltpu.VMEM((frames, 2, tiles, group, LANES), jnp.float32),
             pltpu.VMEM((half + 1, frames, 2, tiles, group, LANES), jnp.float32),
-            dma((CHUNKS,)),
             dma((CHUNKS,)),
             dma((5,)),
             dma((half + 1, n_chan)),

time: 16.9 us -> 16.4 us (0.970)
  Pallas kernels: 15.7 us -> 15.2 us
    pallas_call x1, Pallas kernels: 15.7 us -> 15.2 us  [per_device(): pl.pallas_call(kernel, out_shape=jax.ShapeDtypeStruct((group, 2, half + 1...]
where the time goes in v4:
time: 16.4 us; the launch traced here: 16.3 us
  Pallas kernels  15.2 us (93%)
  local copies, waits for them, and re-layouts  1.06 us (6%)
    pallas_call x1, Pallas kernels, per_device(): pl.pallas_call(kernel, out_shape=jax.ShapeDtypeStruct((group, 2, half + 1...  15.2 us
    unnamed x1, local copies, waits for them, and re-layouts  1.06 us

profile of v4, /device:TPU:0, one launch (start us, length us, event | category | flops | bytes accessed | tf_op | source)
XLA Modules:
  0.0 16.3 jit_solution(8799668608812172127)
XLA Ops:
  0.0 15.2 %correlator.1 = bf16[8,2,5,8,1024]{4,3,2,1,0:T(8,128)(2,1)S(1)} custom-call(s32[8,8]{1,0:T(8,128)} %keeper_ref.1, bf16[2,17,128,128]{3,2,1,0:T(8,128)(2,1)} %bitcast.9, f32[128,128]{1,0:T(8,128)} %constant.8.clone.turn_c_ref, f32[128,128]{1,0:T(8,128)} %constant.9.clone.turn_s_ref, bf16[128,256]{1,0:T(8,128)(2,1)} %constant.10.clone.first_ref, ...), custom_call_target="tpu_custom_call" | custom-call | tf_op jit(solution)/shard_map/correlator/pallas_call | solution.py:458
  15.2 1.1 %copy.9 = bf16[8,2,1024,40]{2,3,1,0:T(8,128)(2,1)} copy(bf16[8,2,1024,40]{2,3,1,0:T(8,128)(2,1)S(1)} %bitcast.8) | data formatting | bytes 2621440

commit v5 on v4

--- a/solution.py
+++ b/solution.py
@@ -231,6 +231,16 @@
             device_id_type=MESH,
         )
 
+    def arrival(d, origin):
+        return pltpu.make_async_remote_copy(
+            src_ref=mine.at[0],
+            dst_ref=parts.at[d, origin],
+            send_sem=send_sem.at[0, 0],
+            recv_sem=recv_sem.at[d, origin],
+            device_id=(pair, chan),
+            device_id_type=MESH,
+        )
+
     def passed(d, origin):
         return pltpu.make_async_remote_copy(
             src_ref=parts.at[d, origin],
@@ -317,6 +327,8 @@
 
     lax.fori_loop(1, half + 1, send_ahead, 0)
     lax.fori_loop(1, half + 1, gate, 0)
+    for step in range(1, n_chan):
+        arrival(0, lax.rem(chan + step, n_chan)).wait_recv()
     lax.fori_loop(1, half + 1, send_late, 0)
 
     away = lax.rem(stn + half, n_stn)
@@ -345,21 +357,15 @@
 
     def receive(k, carry):
         d = at_rank(lax.rem(k, slots))
+        straight_now = k < slots
+        wanted = [comes_straight(d, core) == straight_now for core in range(2)]
+        onward = [straight_now & passes(d, core) for core in range(2)]
         for origin in range(n_chan):
-            here = (d == 0) & (origin == chan)
-
-            @pl.when((comes_straight(d, origin) == (k < slots)) & ~here)
+            @pl.when(wanted[origin % 2] & (d > 0))
             def _():
-                pltpu.make_async_remote_copy(
-                    src_ref=mine.at[0],
-                    dst_ref=parts.at[d, origin],
-                    send_sem=send_sem.at[0, 0],
-                    recv_sem=recv_sem.at[d, origin],
-                    device_id=(pair, chan),
-                    device_id_type=MESH,
-                ).wait_recv()
-
-            @pl.when((k < slots) & passes(d, origin))
+                arrival(d, origin).wait_recv()
+
+            @pl.when(onward[origin % 2])
             def _():
                 passed(d, origin).start()
 
@@ -381,15 +387,17 @@
                 for p in range(2):
                     own[f, p] = others[0, f, p] * (1.0 / frames)
 
-        def slot(s, inner):
-            single = s < base
-            with_far = jnp.where(single, stn - s, half + base - s)
+        def slot(q, inner):
+            single = d < base
+            s = jnp.where(single, stn - d, half + base - d - q)
+            with_far = jnp.where(single, d, d + q)
             unfilled = (s == half) & ~single
             without = jnp.where(single | unfilled, with_far, with_far - 1)
             gain = jnp.where(unfilled, 0.0, 1.0).astype(jnp.float32)
-            ready = jnp.maximum(rank(with_far), rank(without))
-
-            @pl.when(ready == k)
+            other = jnp.where(q == 0, without, with_far)
+            held_slot = jnp.where(single, q == 0, s >= base)
+
+            @pl.when(held_slot & (rank(other) <= k))
             def _():
                 for t in range(tiles):
                     block = [
@@ -409,7 +417,7 @@
 
             return inner
 
-        lax.fori_loop(0, slots, slot, 0)
+        lax.fori_loop(0, 2, slot, 0)
 
     def sent(d, carry):
         @pl.when(straight(stn, chan, d, n_stn))

time: 16.4 us -> 16.1 us (0.982)
  Pallas kernels: 15.2 us -> 14.8 us
    pallas_call x1, Pallas kernels: 15.2 us -> 14.8 us  [per_device(): pl.pallas_call(kernel, out_shape=jax.ShapeDtypeStruct((group, 2, half + 1...]
where the time goes in v5:
time: 16.1 us; the launch traced here: 15.8 us
  Pallas kernels  14.8 us (92%)
  local copies, waits for them, and re-layouts  1.06 us (7%)
    pallas_call x1, Pallas kernels, per_device(): pl.pallas_call(kernel, out_shape=jax.ShapeDtypeStruct((group, 2, half + 1...  14.8 us
    unnamed x1, local copies, waits for them, and re-layouts  1.06 us

profile of v5, /device:TPU:0, one launch (start us, length us, event | category | flops | bytes accessed | tf_op | source)
XLA Modules:
  0.0 15.8 jit_solution(12855806359137287953)
XLA Ops:
  0.0 14.8 %correlator.1 = bf16[8,2,5,8,1024]{4,3,2,1,0:T(8,128)(2,1)S(1)} custom-call(s32[8,8]{1,0:T(8,128)} %keeper_ref.1, bf16[2,17,128,128]{3,2,1,0:T(8,128)(2,1)} %bitcast.9, f32[128,128]{1,0:T(8,128)} %constant.8.clone.turn_c_ref, f32[128,128]{1,0:T(8,128)} %constant.9.clone.turn_s_ref, bf16[128,256]{1,0:T(8,128)(2,1)} %constant.10.clone.first_ref, ...), custom_call_target="tpu_custom_call" | custom-call | tf_op jit(solution)/shard_map/correlator/pallas_call | solution.py:466
  14.8 1.1 %copy.9 = bf16[8,2,1024,40]{2,3,1,0:T(8,128)(2,1)} copy(bf16[8,2,1024,40]{2,3,1,0:T(8,128)(2,1)S(1)} %bitcast.8) | data formatting | bytes 2621440

commit v6 on v5

--- a/solution.py
+++ b/solution.py
@@ -136,14 +136,13 @@
     return planes
 
 
-GATE = 3
 LAST = 2
 
 
-def straight(source, origin, d, n_stn):
+def straight(source, origin, d):
     odd = lax.rem(source, 2) == 1
     odd_d = lax.rem(d, 2) == 1
-    to_even = (source + d >= n_stn) & (d > 2) & (lax.rem(origin, 2) == 0)
+    to_even = (d > 2) & (lax.rem(origin, 2) == 0)
     return (odd & (odd_d == to_even)) | (~odd & (~odd_d | (d == 1))) | (d == 0)
 
 
@@ -251,35 +250,24 @@
             device_id_type=MESH,
         )
 
-    def passes(d, origin):
-        later = d + 1 - 2 * odd
-        source = lax.rem(stn + n_stn - d, n_stn)
-        needed = (d > 0) & (later > 0) & (later <= half)
-        return needed & straight(source, origin, d, n_stn) & ~straight(source, origin, later, n_stn)
+    def passes(d, core):
+        even_d = lax.rem(d, 2) == 0
+        far = (d > 2) & (core == 0)
+        return (d > 1) & jnp.where(odd == 0, (d < half) & (even_d | far), even_d & ~far)
 
     def late(d):
         return stn + d >= n_stn + LAST
 
     def send(d, carry):
-        @pl.when((stn + d >= n_stn) & ~late(d) & straight(stn, chan, d, n_stn))
+        @pl.when((stn + d >= n_stn) & ~late(d) & straight(stn, chan, d))
         def _():
             for step in range(n_chan):
                 direct(d, step).start()
 
         return carry
 
-    def gates(d):
-        return (stn + half >= n_stn + LAST) & (stn + d >= n_stn) & ~late(d) & straight(stn, chan, d, n_stn)
-
-    def gate(d, carry):
-        @pl.when(gates(d))
-        def _():
-            direct(d, GATE).wait_send()
-
-        return carry
-
     def send_late(d, carry):
-        @pl.when(late(d) & straight(stn, chan, d, n_stn))
+        @pl.when(late(d) & straight(stn, chan, d))
         def _():
             for step in range(n_chan):
                 direct(d, step).start()
@@ -291,7 +279,7 @@
         def _():
             pl.semaphore_wait(here_sem.at[d], 1)
 
-            @pl.when(straight(stn, chan, d, n_stn))
+            @pl.when(straight(stn, chan, d))
             def _():
                 for step in range(n_chan):
                     direct(d, step).start()
@@ -302,14 +290,6 @@
     pl.semaphore_wait(barrier, (back + jnp.minimum(stn, half) + 1) * n_chan - 1)
 
 
-    def answer(d, carry):
-        @pl.when(d <= stn)
-        def _():
-            pl.semaphore_signal(here_sem.at[d], inc=1, device_id=(stn - d, chan), device_id_type=MESH)
-
-        return carry
-
-    lax.fori_loop(1, half + 1, answer, 0)
     last = stn + half >= n_stn + LAST
 
     @pl.when(~last)
@@ -325,8 +305,15 @@
     def _():
         lax.fori_loop(1, half + 1, send, 0)
 
+    def answer(d, carry):
+        @pl.when(d <= stn)
+        def _():
+            pl.semaphore_signal(here_sem.at[d], inc=1, device_id=(stn - d, chan), device_id_type=MESH)
+
+        return carry
+
+    lax.fori_loop(1, half + 1, answer, 0)
     lax.fori_loop(1, half + 1, send_ahead, 0)
-    lax.fori_loop(1, half + 1, gate, 0)
     for step in range(1, n_chan):
         arrival(0, lax.rem(chan + step, n_chan)).wait_recv()
     lax.fori_loop(1, half + 1, send_late, 0)
@@ -340,13 +327,11 @@
 
     ahead = jnp.minimum(stn, half)
 
-    def comes_straight(d, origin):
-        return straight(lax.rem(stn + n_stn - d, n_stn), origin, d, n_stn)
+    def comes_straight(d, core):
+        return straight(stn + d, core, d)
 
     def all_straight(d):
-        source = lax.rem(stn + n_stn - d, n_stn)
-        mixed = (lax.rem(source, 2) == 1) & (d > stn) & (d > 2)
-        return ((lax.rem(d, 2) == 0) & ~mixed) | ((lax.rem(source, 2) == 0) & (d == 1))
+        return comes_straight(d, 0) & comes_straight(d, 1)
 
     def rank(d):
         place = jnp.where(d <= ahead, d, half + 1 + ahead - d)
@@ -420,23 +405,19 @@
         lax.fori_loop(0, 2, slot, 0)
 
     def sent(d, carry):
-        @pl.when(straight(stn, chan, d, n_stn))
+        @pl.when(straight(stn, chan, d))
         def _():
             for step in range(n_chan):
-                if step != GATE:
-                    direct(d, step).wait_send()
-
-        @pl.when(straight(stn, chan, d, n_stn) & ~gates(d))
-        def _():
-            direct(d, GATE).wait_send()
+                direct(d, step).wait_send()
 
         return carry
 
     def passed_on(d, carry):
-        for origin in range(n_chan):
-            @pl.when(passes(d, origin))
+        for core in range(2):
+            @pl.when(passes(d, core))
             def _():
-                passed(d, origin).wait_send()
+                for origin in range(core, n_chan, 2):
+                    passed(d, origin).wait_send()
 
         return carry
 

time: 16.1 us -> 16 us (level)
  no operation moved by 1% of the time
where the time goes in v6:
time: 16 us; the launch traced here: 15.9 us
  Pallas kernels  14.8 us (92%)
  local copies, waits for them, and re-layouts  1.06 us (7%)
    pallas_call x1, Pallas kernels, per_device(): pl.pallas_call(kernel, out_shape=jax.ShapeDtypeStruct((group, 2, half + 1...  14.8 us
    unnamed x1, local copies, waits for them, and re-layouts  1.06 us

profile of v6, /device:TPU:0, one launch (start us, length us, event | category | flops | bytes accessed | tf_op | source)
XLA Modules:
  0.0 15.9 jit_solution(12382397335302993055)
XLA Ops:
  0.0 14.8 %correlator.1 = bf16[8,2,5,8,1024]{4,3,2,1,0:T(8,128)(2,1)S(1)} custom-call(s32[8,8]{1,0:T(8,128)} %keeper_ref.1, bf16[2,17,128,128]{3,2,1,0:T(8,128)(2,1)} %bitcast.9, f32[128,128]{1,0:T(8,128)} %constant.8.clone.turn_c_ref, f32[128,128]{1,0:T(8,128)} %constant.9.clone.turn_s_ref, bf16[128,256]{1,0:T(8,128)(2,1)} %constant.10.clone.first_ref, ...), custom_call_target="tpu_custom_call" | custom-call | tf_op jit(solution)/shard_map/correlator/pallas_call | solution.py:447
  14.8 1.1 %copy.9 = bf16[8,2,1024,40]{2,3,1,0:T(8,128)(2,1)} copy(bf16[8,2,1024,40]{2,3,1,0:T(8,128)(2,1)S(1)} %bitcast.8) | data formatting | bytes 2621440

commit v7 on v6

--- a/solution.py
+++ b/solution.py
@@ -290,20 +290,12 @@
     pl.semaphore_wait(barrier, (back + jnp.minimum(stn, half) + 1) * n_chan - 1)
 
 
-    last = stn + half >= n_stn + LAST
-
-    @pl.when(~last)
-    def _():
-        lax.fori_loop(1, half + 1, send, 0)
-
     for step in range(n_chan):
         @pl.when(target(step) != chan)
         def _():
             direct(0, step).start()
 
-    @pl.when(last)
-    def _():
-        lax.fori_loop(1, half + 1, send, 0)
+    lax.fori_loop(1, half + 1, send, 0)
 
     def answer(d, carry):
         @pl.when(d <= stn)

time: 16 us -> 16 us (level)
  no operation moved by 1% of the time
where the time goes in v7:
time: 16 us; the launch traced here: 15.8 us
  Pallas kernels  14.8 us (92%)
  local copies, waits for them, and re-layouts  1.06 us (7%)
    pallas_call x1, Pallas kernels, per_device(): pl.pallas_call(kernel, out_shape=jax.ShapeDtypeStruct((group, 2, half + 1...  14.8 us
    unnamed x1, local copies, waits for them, and re-layouts  1.06 us

profile of v7, /device:TPU:0, one launch (start us, length us, event | category | flops | bytes accessed | tf_op | source)
XLA Modules:
  0.0 15.8 jit_solution(182312154385550228)
XLA Ops:
  0.0 14.8 %correlator.1 = bf16[8,2,5,8,1024]{4,3,2,1,0:T(8,128)(2,1)S(1)} custom-call(s32[8,8]{1,0:T(8,128)} %keeper_ref.1, bf16[2,17,128,128]{3,2,1,0:T(8,128)(2,1)} %bitcast.9, f32[128,128]{1,0:T(8,128)} %constant.8.clone.turn_c_ref, f32[128,128]{1,0:T(8,128)} %constant.9.clone.turn_s_ref, bf16[128,256]{1,0:T(8,128)(2,1)} %constant.10.clone.first_ref, ...), custom_call_target="tpu_custom_call" | custom-call | tf_op jit(solution)/shard_map/correlator/pallas_call | solution.py:439
  14.8 1.1 %copy.9 = bf16[8,2,1024,40]{2,3,1,0:T(8,128)(2,1)} copy(bf16[8,2,1024,40]{2,3,1,0:T(8,128)(2,1)S(1)} %bitcast.8) | data formatting | bytes 2621440
